TPU v7x, 32 devices: a whole 2x2x4 slice. The times are simulated.
32 devices in a mesh: ctx: 8 (over y, x, core), dp: 4 (over z).
Axes of the slice: x: 2, y: 2, z: 4, core: 2. Of those that a mesh axis runs over, the one named last changes fastest.
Arguments:
- hidden_in: bfloat16 [4, 2048, 2048], P('dp', 'ctx'), may hold values from -6 to 6
- queries: bfloat16 [4, 2048, 2048], P('dp', 'ctx'), may hold values from -1000 to 1000
- norm_gain: bfloat16 [2048], replicated, may hold values from 0.099609375 to 1.8984375
- weight_store: bfloat16 [4, 2048, 512], P('dp', 'ctx'), may hold values from -0.125 to 0.125
- owners: int32 [2], replicated, may hold values from 0 to 3, as said below
- doc_lengths: int32 [4, 4], P('dp'), may hold values from 1 to 1024, 2048 in all within a row
Outputs:
- attended: bfloat16 [4, 2048, 2048], P('dp', 'ctx')
Inputs may be any that keep to these rules, and one draw needn't show every extreme that they name: `owners`: two different data ranks, one of them the last rank 4 - 1; the first owns the key projection, the second the value projection.
All inputs are finite; a program needn't handle non-finite values.
Results may differ from a plain program's by a relative error of at most 0.012.
Values may be sent and summed in bfloat16 or wider, within the bound.
No kernel may reach another device: no remote copies, remote signals or barrier semaphores. Data moves between devices by JAX's collectives and lax.ppermute only.
A program may use at most 64 MiB of HBM per device.

v0:
```python
import jax
import jax.numpy as jnp
from jax import lax
from jax.sharding import PartitionSpec as P

HS = 128
REACH = 4


def from_root(block, axis, owner):
    block = jnp.where(lax.axis_index(axis) == owner, block, jnp.zeros_like(block))
    return lax.psum(block, axis)


def from_behind(x, axis, by):
    size = lax.axis_size(axis)
    pairs = [(i, i + by) for i in range(size) if 0 <= i + by < size]
    return lax.ppermute(x, axis, pairs)


def find_starts(lengths, positions):
    ends = jnp.cumsum(lengths)
    starts = ends - lengths
    below = starts[None, :] <= positions[:, None]
    return jnp.max(jnp.where(below, starts[None, :], 0), axis=1)


def copy_owner(slot_rows, owner):
    return from_root(slot_rows, "dp", owner)


def local(hidden_in, queries, norm_gain, weight_store, owners, doc_lengths):
    tok_rows = hidden_in.shape[1]
    key_width = weight_store.shape[2]
    kv_heads = key_width // HS
    group = queries.shape[2] // key_width
    width_all = (REACH + 1) * tok_rows
    ctx_index = lax.axis_index("ctx")
    xf = hidden_in[0].astype(jnp.float32)
    scaled = (
        xf
        * lax.rsqrt(jnp.mean(xf * xf, axis=-1, keepdims=True) + 1e-05)
        * norm_gain.astype(jnp.float32)
    ).astype(jnp.bfloat16)
    own_slot = weight_store[0]
    key_part = copy_owner(own_slot, owners[0])
    value_part = copy_owner(own_slot, owners[1])
    key_sum = jnp.dot(
        scaled,
        lax.all_gather(key_part, "ctx", axis=0, tiled=True),
        preferred_element_type=jnp.float32,
    )
    value_sum = jnp.dot(
        scaled,
        lax.all_gather(value_part, "ctx", axis=0, tiled=True),
        preferred_element_type=jnp.float32,
    )
    kv_own = jnp.stack([key_sum.astype(jnp.bfloat16), value_sum.astype(jnp.bfloat16)])
    earlier = [from_behind(kv_own, "ctx", back) for back in range(REACH, 0, -1)]
    window = jnp.concatenate(earlier + [kv_own], axis=1)
    q_pos = ctx_index * tok_rows + jnp.arange(tok_rows, dtype=jnp.int32)
    k_pos = (ctx_index - REACH) * tok_rows + jnp.arange(width_all, dtype=jnp.int32)
    q_start = find_starts(doc_lengths[0], q_pos)
    allowed = (k_pos[None, :] >= q_start[:, None]) & (k_pos[None, :] <= q_pos[:, None])
    q_heads = jnp.transpose(queries[0].reshape(tok_rows, kv_heads, group, HS), (1, 2, 0, 3))
    k_heads = jnp.transpose(window[0].reshape(width_all, kv_heads, HS), (1, 0, 2))
    v_heads = jnp.transpose(window[1].reshape(width_all, kv_heads, HS), (1, 0, 2))
    inverse_root = 1.0 / jnp.sqrt(jnp.float32(HS))

    def one_head(args):
        q_one, k_one, v_one = args
        rows = q_one.reshape(group * tok_rows, HS)
        score = jnp.dot(rows, k_one.T, preferred_element_type=jnp.float32)
        score = score.reshape(group, tok_rows, width_all) * inverse_root
        score = jnp.where(allowed[None], score, jnp.float32(-1e30))
        top = jnp.max(score, axis=-1, keepdims=True)
        weight = jnp.exp(score - top)
        total = jnp.sum(weight, axis=-1)
        weight_b = weight.astype(jnp.bfloat16).reshape(group * tok_rows, width_all)
        summed = jnp.dot(weight_b, v_one, preferred_element_type=jnp.float32)
        summed = summed.reshape(group, tok_rows, HS)
        return (summed / total[..., None]).astype(jnp.bfloat16)

    outputs = lax.map(one_head, (q_heads, k_heads, v_heads))
    attended = jnp.transpose(outputs, (2, 0, 1, 3)).reshape(1, tok_rows, kv_heads * group * HS)
    return attended


def solution(mesh):
    return jax.shard_map(
        local,
        mesh=mesh,
        in_specs=(
            P("dp", "ctx", None),
            P("dp", "ctx", None),
            P(),
            P("dp", "ctx", None),
            P(),
            P("dp", None),
        ),
        out_specs=P("dp", "ctx", None),
        check_vma=False,
    )
```

profile of v0, /device:TPU:1, one launch (start us, length us, event | category | flops | bytes accessed | tf_op | source)
XLA Modules:
  0.0 198.7 jit_solution(8778680894563662250)
XLA Ops:
  6.5 1.4 fusion.36
  9.3 1.8 select_bitcast_fusion.1
  11.1 39.7 %all-reduce.3.cloned.1.call-done = (bf16[256,512]{1,0:T(8,128)(2,1)}, bf16[256,512]{1,0:T(8,128)(2,1)}) async-done(((bf16[256,512]{1,0:T(8,128)(2,1)}, bf16[256,512]{1,0:T(8,128)(2,1)}), (bf16[256,512]{1,0:T(8,128)(2,1)}, bf16[256,512]{1,0:T(8,128)(2,1)})) %all-reduce.3.cloned.1.call-update) | async-done | bytes 524304 | tf_op jit(solution)/shard_map/psum | solution.py:12
  50.9 0.7 all-gather.5.cloned.1.call-update
  51.6 0.7 convert_element_type.26
  52.2 0.8 reduce-window_clone.1
  53.1 0.3 fusion.27
  53.4 28.6 %all-gather.3.cloned.1.call-done = bf16[2048,512]{1,0:T(8,128)(2,1)} async-done(((bf16[256,512]{1,0:T(8,128)(2,1)}), bf16[2048,512]{1,0:T(8,128)(2,1)}) %all-gather.3.cloned.1.call-update) | async-done | bytes 2097168 | tf_op jit(solution)/shard_map/all_gather | solution.py:50
  82.0 2.3 %fusion.30 = bf16[1,256,512]{2,1,0:T(8,128)(2,1)S(1)} fusion(bf16[2048,512]{1,0:T(8,128)(2,1)} %all-gather.3.cloned.1.call-done, bf16[1,256,2048]{2,1,0:T(8,128)(2,1)S(1)} %copy-done, f32[2048]{0:T(1024)S(1)} %convert_element_type.26, f32[256]{0:T(256)S(1)} %add_rsqrt_fusion), kind=kOutput, calls=%fused_computation.29 | convolution fusion | flops 539099136 | bytes 3417088 | tf_op jit(solution)/shard_map/dot_general | solution.py:48
  84.4 27.5 %all-gather.5.cloned.1.call-done = bf16[2048,512]{1,0:T(8,128)(2,1)} async-done(((bf16[256,512]{1,0:T(8,128)(2,1)}), bf16[2048,512]{1,0:T(8,128)(2,1)}) %all-gather.5.cloned.1.call-update) | async-done | bytes 2097168 | tf_op jit(solution)/shard_map/all_gather | solution.py:55
  111.8 2.3 %fusion.31 = bf16[1,256,512]{2,1,0:T(8,128)(2,1)S(1)} fusion(bf16[2048,512]{1,0:T(8,128)(2,1)} %all-gather.5.cloned.1.call-done, bf16[1,256,2048]{2,1,0:T(8,128)(2,1)S(1)} %copy-done, f32[2048]{0:T(1024)S(1)} %convert_element_type.26, f32[256]{0:T(256)S(1)} %add_rsqrt_fusion), kind=kOutput, calls=%fused_computation.30 | convolution fusion | flops 539099136 | bytes 3417088 | tf_op jit(solution)/shard_map/dot_general | solution.py:53
  114.2 0.7 copy-done.2
  114.9 0.8 pad_maximum_fusion
  115.7 3.8 %collective-permute-start = (bf16[2,256,512]{2,1,0:T(8,128)(2,1)}, bf16[2,256,512]{2,1,0:T(8,128)(2,1)}, u32[]{:S(2)}, u32[]{:S(2)}) collective-permute-start(bf16[2,256,512]{2,1,0:T(8,128)(2,1)} %pad_maximum_fusion), channel_id=1, source_target_pairs={{0,16},{4,20},{8,24},{12,28},{1,17},{5,21},{9,25},{13,29},{2,18},{... | collective-permute-start | bytes 1572872 | tf_op jit(solution)/shard_map/ppermute | solution.py:18
  119.5 2.1 %collective-permute-start.1 = (bf16[2,256,512]{2,1,0:T(8,128)(2,1)}, bf16[2,256,512]{2,1,0:T(8,128)(2,1)}, u32[]{:S(2)}, u32[]{:S(2)}) collective-permute-start(bf16[2,256,512]{2,1,0:T(8,128)(2,1)} %pad_maximum_fusion), channel_id=1, source_target_pairs={{0,12},{4,16},{8,20},{12,24},{16,28},{1,13},{5,17},{9,21},{13,25},... | collective-permute-start | bytes 1572872 | tf_op jit(solution)/shard_map/ppermute | solution.py:18
  121.6 2.9 %collective-permute-start.2 = (bf16[2,256,512]{2,1,0:T(8,128)(2,1)}, bf16[2,256,512]{2,1,0:T(8,128)(2,1)}, u32[]{:S(2)}, u32[]{:S(2)}) collective-permute-start(bf16[2,256,512]{2,1,0:T(8,128)(2,1)} %pad_maximum_fusion), channel_id=1, source_target_pairs={{0,8},{4,12},{8,16},{12,20},{16,24},{20,28},{1,9},{5,13},{9,17},{1... | collective-permute-start | bytes 1572872 | tf_op jit(solution)/shard_map/ppermute | solution.py:18
  124.5 1.9 collective-permute-start.3
  126.5 0.5 copy.15
  127.0 0.1 select_reduce_fusion
  127.1 25.4 %collective-permute-done = bf16[2,256,512]{2,1,0:T(8,128)(2,1)} collective-permute-done((bf16[2,256,512]{2,1,0:T(8,128)(2,1)}, bf16[2,256,512]{2,1,0:T(8,128)(2,1)}, u32[]{:S(2)}, u32[]{:S(2)}) %collective-permute-start) | collective-permute-done | bytes 524320 | tf_op jit(solution)/shard_map/ppermute | solution.py:18
  152.5 1.1 constant_dynamic-update-slice_fusion.4
  153.6 5.2 %collective-permute-done.1 = bf16[2,256,512]{2,1,0:T(8,128)(2,1)} collective-permute-done((bf16[2,256,512]{2,1,0:T(8,128)(2,1)}, bf16[2,256,512]{2,1,0:T(8,128)(2,1)}, u32[]{:S(2)}, u32[]{:S(2)}) %collective-permute-start.1) | collective-permute-done | bytes 524320 | tf_op jit(solution)/shard_map/ppermute | solution.py:18
  158.8 1.1 constant_dynamic-update-slice_fusion.3
  159.9 1.1 constant_dynamic-update-slice_fusion.2
  161.0 1.1 constant_dynamic-update-slice_fusion.1
  162.1 1.2 fusion.35
  163.4 3.6 %reshape_squeeze.10 = bf16[1280,4,128]{2,1,0:T(4,128)(2,1)} reshape(bf16[1,1280,512]{2,1,0:T(8,128)(2,1)} %get-tuple-element.96) | data formatting | bytes 2621440 | tf_op jit(solution)/shard_map/reshape;squeeze | solution.py:66
  166.9 1.2 reshape_squeeze.11
  168.2 3.1 %copy_bitcast_fusion = (bf16[4,1280,128]{2,1,0:T(8,128)(2,1)}, bf16[4,1280,128]{2,1,0:T(8,128)(2,1)S(1)}) fusion(bf16[1280,4,128]{2,1,0:T(4,128)(2,1)} %reshape_squeeze.11, bf16[1280,4,128]{2,1,0:T(4,128)(2,1)} %reshape_squeeze.10), kind=kLoop, calls=%fused_computation.25 | loop fusion | bytes 5242880 | tf_op jit(solution)/shard_map/transpose | solution.py:67
  171.3 18.5 %while.11 = (s32[]{:T(128)}, bf16[4,4,256,128]{3,2,1,0:T(8,128)(2,1)S(1)}, bf16[4,4,256,128]{2,3,1,0:T(8,128)(2,1)S(1)}, bf16[4,1280,128]{2,1,0:T(8,128)(2,1)S(1...) while((s32[]{:T(128)}, ...), condition=%wide.region_8.9_spmd.clone, body=%wide.region_5.8_spmd.clone.sunk | while | flops 681506816 | bytes 17593436 | solution.py:84
  171.3 0.3 compare_and_fusion.2
  171.6 1.3 fusion.46
  172.9 1.0 fusion.47
  173.9 2.0 %fusion.48 = bf16[4,4,256,128]{3,2,1,0:T(8,128)(2,1)S(1)} fusion(bf16[4,4,256,128]{3,2,1,0:T(8,128)(2,1)S(1)} %get-tuple-element.166, s32[]{:T(128)} %get-tuple-element.165, f32[4,256,1280]{2,1,0:T(8,128)S(1)} %get-tuple-element.154, f32[4,256]{1,0:T(4,128)S(1)} %get-tuple-element.155, bf16[4,1280,128]{2,1,0:T(8,128)(2,1)} %get-tuple-element.178, ...), kind=kOutput, calls=%fused_computation.11.clone.1 | convolution fusion | flops 338427904 | bytes 5841920 | tf_op jit(solution)/shard_map/while/body/eval_jaxpr/dot_general | solution.py:80
  175.9 0.3 compare_and_fusion.2
  176.2 1.3 fusion.46
  177.5 1.0 fusion.47
  178.5 2.0 %fusion.48 = bf16[4,4,256,128]{3,2,1,0:T(8,128)(2,1)S(1)} fusion(bf16[4,4,256,128]{3,2,1,0:T(8,128)(2,1)S(1)} %get-tuple-element.166, s32[]{:T(128)} %get-tuple-element.165, f32[4,256,1280]{2,1,0:T(8,128)S(1)} %get-tuple-element.154, f32[4,256]{1,0:T(4,128)S(1)} %get-tuple-element.155, bf16[4,1280,128]{2,1,0:T(8,128)(2,1)} %get-tuple-element.178, ...), kind=kOutput, calls=%fused_computation.11.clone.1 | convolution fusion | flops 338427904 | bytes 5841920 | tf_op jit(solution)/shard_map/while/body/eval_jaxpr/dot_general | solution.py:80
  180.5 0.3 compare_and_fusion.2
  180.8 1.3 fusion.46
  182.1 1.0 fusion.47
  183.1 2.0 %fusion.48 = bf16[4,4,256,128]{3,2,1,0:T(8,128)(2,1)S(1)} fusion(bf16[4,4,256,128]{3,2,1,0:T(8,128)(2,1)S(1)} %get-tuple-element.166, s32[]{:T(128)} %get-tuple-element.165, f32[4,256,1280]{2,1,0:T(8,128)S(1)} %get-tuple-element.154, f32[4,256]{1,0:T(4,128)S(1)} %get-tuple-element.155, bf16[4,1280,128]{2,1,0:T(8,128)(2,1)} %get-tuple-element.178, ...), kind=kOutput, calls=%fused_computation.11.clone.1 | convolution fusion | flops 338427904 | bytes 5841920 | tf_op jit(solution)/shard_map/while/body/eval_jaxpr/dot_general | solution.py:80
  185.1 0.3 compare_and_fusion.2
  185.5 1.3 fusion.46
  186.8 1.0 fusion.47
  187.7 2.0 %fusion.48 = bf16[4,4,256,128]{3,2,1,0:T(8,128)(2,1)S(1)} fusion(bf16[4,4,256,128]{3,2,1,0:T(8,128)(2,1)S(1)} %get-tuple-element.166, s32[]{:T(128)} %get-tuple-element.165, f32[4,256,1280]{2,1,0:T(8,128)S(1)} %get-tuple-element.154, f32[4,256]{1,0:T(4,128)S(1)} %get-tuple-element.155, bf16[4,1280,128]{2,1,0:T(8,128)(2,1)} %get-tuple-element.178, ...), kind=kOutput, calls=%fused_computation.11.clone.1 | convolution fusion | flops 338427904 | bytes 5841920 | tf_op jit(solution)/shard_map/while/body/eval_jaxpr/dot_general | solution.py:80
  189.7 0.8 copy.19
  190.6 1.6 reshape.47
  (22 shorter events, 0.2 us)
Async XLA Ops:
  6.5 46.5 %copy-start = (bf16[1,256,2048]{2,1,0:T(8,128)(2,1)S(1)}, bf16[1,256,2048]{2,1,0:T(8,128)(2,1)}, u32[]{:S(2)}) copy-start(bf16[1,256,2048]{2,1,0:T(8,128)(2,1)} %param.8) | copy-start | bytes 3145732
  6.5 44.3 %all-reduce.3.cloned.1.call-start = ((), (), s32[]{:S(2)}) async-start(), calls=%async_computation.2 | async-start | bytes 1048576 | tf_op jit(solution)/shard_map/psum | solution.py:12
  11.1 70.9 %all-gather.3.cloned.1.call-start = ((), (), s32[]{:S(2)}) async-start(), calls=%async_computation | async-start | bytes 2359296 | tf_op jit(solution)/shard_map/all_gather | solution.py:50
  50.8 61.0 %all-gather.5.cloned.1.call-start = ((), (), s32[]{:S(2)}) async-start(), calls=%async_computation.1 | async-start | bytes 2359296 | tf_op jit(solution)/shard_map/all_gather | solution.py:55
  84.3 37.3 %copy-start.4 = (s32[1,4]{1,0:T(1,128)S(1)}, s32[1,4]{1,0:T(1,128)}, u32[]{:S(2)}) copy-start(s32[1,4]{1,0:T(1,128)} %param.13) | copy-start | bytes 52
  84.3 42.1 %copy-start.1 = (bf16[1,256,2048]{2,1,0:T(8,128)(2,1)S(1)}, bf16[1,256,2048]{2,1,0:T(8,128)(2,1)}, u32[]{:S(2)}) copy-start(bf16[1,256,2048]{2,1,0:T(8,128)(2,1)} %param.9) | copy-start | bytes 3145732
  114.2 0.7 copy-start.2
  115.7 36.8 %collective-permute-start = (bf16[2,256,512]{2,1,0:T(8,128)(2,1)}, bf16[2,256,512]{2,1,0:T(8,128)(2,1)}, u32[]{:S(2)}, u32[]{:S(2)}) collective-permute-start(bf16[2,256,512]{2,1,0:T(8,128)(2,1)} %pad_maximum_fusion), channel_id=1, source_target_pairs={{0,16},{4,20},{8,24},{12,28},{1,17},{5,21},{9,25},{13,29},{2,18},{... | collective-permute-start | bytes 1572872 | tf_op jit(solution)/shard_map/ppermute | solution.py:18
  119.5 39.3 %collective-permute-start.1 = (bf16[2,256,512]{2,1,0:T(8,128)(2,1)}, bf16[2,256,512]{2,1,0:T(8,128)(2,1)}, u32[]{:S(2)}, u32[]{:S(2)}) collective-permute-start(bf16[2,256,512]{2,1,0:T(8,128)(2,1)} %pad_maximum_fusion), channel_id=1, source_target_pairs={{0,12},{4,16},{8,20},{12,24},{16,28},{1,13},{5,17},{9,21},{13,25},... | collective-permute-start | bytes 1572872 | tf_op jit(solution)/shard_map/ppermute | solution.py:18
  121.6 38.3 %collective-permute-start.2 = (bf16[2,256,512]{2,1,0:T(8,128)(2,1)}, bf16[2,256,512]{2,1,0:T(8,128)(2,1)}, u32[]{:S(2)}, u32[]{:S(2)}) collective-permute-start(bf16[2,256,512]{2,1,0:T(8,128)(2,1)} %pad_maximum_fusion), channel_id=1, source_target_pairs={{0,8},{4,12},{8,16},{12,20},{16,24},{20,28},{1,9},{5,13},{9,17},{1... | collective-permute-start | bytes 1572872 | tf_op jit(solution)/shard_map/ppermute | solution.py:18
  124.5 36.5 %collective-permute-start.3 = (bf16[2,256,512]{2,1,0:T(8,128)(2,1)}, bf16[2,256,512]{2,1,0:T(8,128)(2,1)}, u32[]{:S(2)}, u32[]{:S(2)}) collective-permute-start(bf16[2,256,512]{2,1,0:T(8,128)(2,1)} %pad_maximum_fusion), channel_id=1, source_target_pairs={{0,4},{4,8},{8,12},{12,16},{16,20},{20,24},{24,28},{1,5},{5,9},{9,... | collective-permute-start | bytes 1572872 | tf_op jit(solution)/shard_map/ppermute | solution.py:18
  127.1 35.0 %copy-start.3 = (bf16[1,256,512]{2,1,0:T(8,128)(2,1)S(1)}, bf16[1,256,512]{2,1,0:T(8,128)(2,1)}, u32[]{:S(2)}) copy-start(bf16[1,256,512]{2,1,0:T(8,128)(2,1)} %copy-done.2) | copy-start | bytes 786436
Sparse Core Ops, SparseCore 0:
  11.2 39.5 all-reduce.2
  52.7 29.2 all-gather.2
  83.9 27.8 all-gather.4
where the time goes:
time: 199 us
  waiting for transfers between devices  127 us (64%)
  local copies, waits for them, and re-layouts  18.5 us (9%)
  matrix products  17.9 us (9%)
  between operations  14.6 us (7%)
  starting transfers between devices  10.8 us (5%)
  other arithmetic  9.72 us (5%)
    psum x1, waiting for transfers between devices, from_root(): return lax.psum(block, axis)  39.7 us
    ppermute x4, waiting for transfers between devices, from_behind(): return lax.ppermute(x, axis, pairs)  30.6 us
    all_gather x1, waiting for transfers between devices, local(): lax.all_gather(key_part, 'ctx', axis=0, tiled=True)  28.6 us
    all_gather x1, waiting for transfers between devices, local(): lax.all_gather(value_part, 'ctx', axis=0, tiled=True)  27.5 us
    ppermute x4, starting transfers between devices, from_behind(): return lax.ppermute(x, axis, pairs)  10.7 us
    dot_general x4, matrix products, one_head(): summed = jnp.dot(weight_b, v_one, preferred_element_type=jnp.float32)  8.07 us
    unnamed x15, local copies, waits for them, and re-layouts  5.55 us
    dot_general x4, matrix products, one_head(): score = jnp.dot(rows, k_one.T, preferred_element_type=jnp.float32)  5.14 us
  transfers between devices with their start and end apart: 7, of which 5 were waited for; matrix products, arithmetic and copies ran while one was open for 4% of the time, Pallas kernels for 0%

commit v1 on v0

--- a/solution.py
+++ b/solution.py
@@ -45,11 +45,21 @@
     own_slot = weight_store[0]
     key_part = copy_owner(own_slot, owners[0])
     value_part = copy_owner(own_slot, owners[1])
-    key_sum = jnp.dot(
-        scaled,
-        lax.all_gather(key_part, "ctx", axis=0, tiled=True),
-        preferred_element_type=jnp.float32,
-    )
+
+    def keep_up_heads_for(body):
+        p_next = lax.axis_size("ctx")
+        then = lax.axis_index("ctx")
+        piece_now, g_now = (p_next, then)
+        s_next, far_arr = (body, 1)
+        while far_arr < piece_now:
+            block_out = lax.ppermute(s_next, "ctx", [(pp, pp ^ far_arr) for pp in range(piece_now)])
+            u1 = jnp.concatenate([s_next, block_out], axis=0)
+            view_out = jnp.concatenate([block_out, s_next], axis=0)
+            s_next = jnp.where(g_now & far_arr == 0, u1, view_out)
+            far_arr = 2 * far_arr
+        return s_next
+
+    key_sum = jnp.dot(scaled, keep_up_heads_for(key_part), preferred_element_type=jnp.float32)
     value_sum = jnp.dot(
         scaled,
         lax.all_gather(value_part, "ctx", axis=0, tiled=True),

time: 199 us -> 190 us (0.955)
  waiting for transfers between devices: 127 us -> 110 us
  starting transfers between devices: 10.8 us -> 17.7 us
    ppermute x0 -> x3, waiting for transfers between devices: none -> 43.6 us  [keep_up_heads_for(): lax.ppermute(s_next, 'ctx', [(pp, pp ^ far_arr) for pp in range(piece_now)])]
    all_gather x1 -> x0, waiting for transfers between devices: 28.6 us -> none  [local(): lax.all_gather(key_part, 'ctx', axis=0, tiled=True)]
    all_gather x1, waiting for transfers between devices: 27.5 us -> 0.02 us  [local(): lax.all_gather(value_part, 'ctx', axis=0, tiled=True)]
    ppermute x0 -> x3, starting transfers between devices: none -> 4.3 us  [keep_up_heads_for(): lax.ppermute(s_next, 'ctx', [(pp, pp ^ far_arr) for pp in range(piece_now)])]
    ppermute x4, waiting for transfers between devices: 30.6 us -> 26.9 us  [from_behind(): return lax.ppermute(x, axis, pairs)]
    ppermute x4, starting transfers between devices: 10.7 us -> 13.3 us  [from_behind(): return lax.ppermute(x, axis, pairs)]
  transfers between devices with their start and end apart: 7 -> 9, of which waited for: 5 -> 6; matrix products, arithmetic and copies ran while one was open for 4% -> 5% of each run, Pallas kernels for 0% -> 0%
where the time goes in v1:
time: 190 us; the launch traced here: 189 us
  waiting for transfers between devices  110 us (58%)
  local copies, waits for them, and re-layouts  18.7 us (10%)
  matrix products  18.1 us (10%)
  starting transfers between devices  17.7 us (9%)
  between operations  14.9 us (8%)
  other arithmetic  9.22 us (5%)
    ppermute x3, waiting for transfers between devices, keep_up_heads_for(): lax.ppermute(s_next, 'ctx', [(pp, pp ^ far_arr) for pp in range(piece_now)])  43.6 us
    psum x1, waiting for transfers between devices, from_root(): return lax.psum(block, axis)  39.7 us
    ppermute x4, waiting for transfers between devices, from_behind(): return lax.ppermute(x, axis, pairs)  26.9 us
    ppermute x4, starting transfers between devices, from_behind(): return lax.ppermute(x, axis, pairs)  13.3 us
    dot_general x4, matrix products, one_head(): summed = jnp.dot(weight_b, v_one, preferred_element_type=jnp.float32)  8.07 us
    unnamed x15, local copies, waits for them, and re-layouts  5.81 us
    dot_general x4, matrix products, one_head(): score = jnp.dot(rows, k_one.T, preferred_element_type=jnp.float32)  5.14 us
    ppermute x3, starting transfers between devices, keep_up_heads_for(): lax.ppermute(s_next, 'ctx', [(pp, pp ^ far_arr) for pp in range(piece_now)])  4.3 us
  transfers between devices with their start and end apart: 9, of which 6 were waited for; matrix products, arithmetic and copies ran while one was open for 5% of the time, Pallas kernels for 0%

profile of v1, /device:TPU:1, one launch (start us, length us, event | category | flops | bytes accessed | tf_op | source)
XLA Modules:
  0.0 188.9 jit_solution(4720363850718230239)
XLA Ops:
  6.5 1.4 fusion.45
  9.3 1.8 select_bitcast_fusion.1
  11.1 39.7 %all-reduce.3.cloned.1.call-done = (bf16[256,512]{1,0:T(8,128)(2,1)}, bf16[256,512]{1,0:T(8,128)(2,1)}) async-done(((bf16[256,512]{1,0:T(8,128)(2,1)}, bf16[256,512]{1,0:T(8,128)(2,1)}), (bf16[256,512]{1,0:T(8,128)(2,1)}, bf16[256,512]{1,0:T(8,128)(2,1)})) %all-reduce.3.cloned.1.call-update) | async-done | bytes 524304 | tf_op jit(solution)/shard_map/psum | solution.py:12
  50.8 1.7 collective-permute-start
  52.6 1.4 collective-permute-done
  53.9 1.2 maximum_select_fusion.7
  55.1 1.3 collective-permute-start.1
  56.4 14.7 %collective-permute-done.1 = bf16[512,512]{1,0:T(8,128)(2,1)S(1)} collective-permute-done((bf16[512,512]{1,0:T(8,128)(2,1)S(1)}, bf16[512,512]{1,0:T(8,128)(2,1)S(1)}, u32[]{:S(2)}, u32[]{:S(2)}) %collective-permute-start.1) | collective-permute-done | bytes 524320 | tf_op jit(solution)/shard_map/ppermute | solution.py:55
  71.1 0.5 maximum_select_fusion.6
  71.6 1.3 collective-permute-start.2
  73.0 0.3 fusion.27
  73.3 27.5 %collective-permute-done.2 = bf16[1024,512]{1,0:T(8,128)(2,1)} collective-permute-done((bf16[1024,512]{1,0:T(8,128)(2,1)S(1)}, bf16[1024,512]{1,0:T(8,128)(2,1)}, u32[]{:S(2)}, u32[]{:S(2)}) %collective-permute-start.2) | collective-permute-done | bytes 1048608 | tf_op jit(solution)/shard_map/ppermute | solution.py:55
  100.8 2.4 %fusion.38 = bf16[1,256,512]{2,1,0:T(8,128)(2,1)S(1)} fusion(bf16[1024,512]{1,0:T(8,128)(2,1)} %collective-permute-done.2, bf16[1024,512]{1,0:T(8,128)(2,1)S(1)} %maximum_select_fusion.6, pred[]{:T(512)S(6)} %eq.15, bf16[1,256,2048]{2,1,0:T(8,128)(2,1)S(1)} %copy-done, f32[2048]{0:T(1024)S(1)} %convert_element_type.26, f32[256]{0:T(256)S(1)} %add_rsqrt_fusion), kind=kOutput, calls=%fused_computation.37 | convolution fusion | flops 548536320 | bytes 3417089 | tf_op jit(solution)/shard_map/dot_general | solution.py:62
  103.3 2.4 %fusion.39 = bf16[1,256,512]{2,1,0:T(8,128)(2,1)S(1)} fusion(bf16[2048,512]{1,0:T(8,128)(2,1)} %all-gather.2.cloned.1.call-done, bf16[1,256,2048]{2,1,0:T(8,128)(2,1)S(1)} %copy-done, f32[2048]{0:T(1024)S(1)} %convert_element_type.26, f32[256]{0:T(256)S(1)} %add_rsqrt_fusion), kind=kOutput, calls=%fused_computation.38 | convolution fusion | flops 539099136 | bytes 3417088 | tf_op jit(solution)/shard_map/dot_general | solution.py:63
  105.8 3.9 %collective-permute-start.3 = (bf16[2,256,512]{2,1,0:T(8,128)(2,1)S(1)}, bf16[2,256,512]{2,1,0:T(8,128)(2,1)}, u32[]{:S(2)}, u32[]{:S(2)}) collective-permute-start(bf16[2,256,512]{2,1,0:T(8,128)(2,1)S(1)} %pad_maximum_fusion), channel_id=1, source_target_pairs={{0,16},{4,20},{8,24},{12,28},{1,17},{5,21},{9,25},{13,29},{2,18},{... | collective-permute-start | bytes 1572872 | tf_op jit(solution)/shard_map/ppermute | solution.py:18
  109.7 3.3 %collective-permute-start.4 = (bf16[2,256,512]{2,1,0:T(8,128)(2,1)S(1)}, bf16[2,256,512]{2,1,0:T(8,128)(2,1)}, u32[]{:S(2)}, u32[]{:S(2)}) collective-permute-start(bf16[2,256,512]{2,1,0:T(8,128)(2,1)S(1)} %pad_maximum_fusion), channel_id=1, source_target_pairs={{0,12},{4,16},{8,20},{12,24},{16,28},{1,13},{5,17},{9,21},{13,25},... | collective-permute-start | bytes 1572872 | tf_op jit(solution)/shard_map/ppermute | solution.py:18
  113.0 3.1 %collective-permute-start.5 = (bf16[2,256,512]{2,1,0:T(8,128)(2,1)S(1)}, bf16[2,256,512]{2,1,0:T(8,128)(2,1)}, u32[]{:S(2)}, u32[]{:S(2)}) collective-permute-start(bf16[2,256,512]{2,1,0:T(8,128)(2,1)S(1)} %pad_maximum_fusion), channel_id=1, source_target_pairs={{0,8},{4,12},{8,16},{12,20},{16,24},{20,28},{1,9},{5,13},{9,17},{1... | collective-permute-start | bytes 1572872 | tf_op jit(solution)/shard_map/ppermute | solution.py:18
  116.1 3.0 %collective-permute-start.6 = (bf16[2,256,512]{2,1,0:T(8,128)(2,1)S(1)}, bf16[2,256,512]{2,1,0:T(8,128)(2,1)}, u32[]{:S(2)}, u32[]{:S(2)}) collective-permute-start(bf16[2,256,512]{2,1,0:T(8,128)(2,1)S(1)} %pad_maximum_fusion), channel_id=1, source_target_pairs={{0,4},{4,8},{8,12},{12,16},{16,20},{20,24},{24,28},{1,5},{5,9},{9,... | collective-permute-start | bytes 1572872 | tf_op jit(solution)/shard_map/ppermute | solution.py:18
  119.1 1.5 copy.15
  120.7 19.7 %collective-permute-done.3 = bf16[2,256,512]{2,1,0:T(8,128)(2,1)} collective-permute-done((bf16[2,256,512]{2,1,0:T(8,128)(2,1)S(1)}, bf16[2,256,512]{2,1,0:T(8,128)(2,1)}, u32[]{:S(2)}, u32[]{:S(2)}) %collective-permute-start.3) | collective-permute-done | bytes 524320 | tf_op jit(solution)/shard_map/ppermute | solution.py:18
  140.4 1.1 constant_dynamic-update-slice_fusion.4
  141.5 7.2 %collective-permute-done.4 = bf16[2,256,512]{2,1,0:T(8,128)(2,1)} collective-permute-done((bf16[2,256,512]{2,1,0:T(8,128)(2,1)S(1)}, bf16[2,256,512]{2,1,0:T(8,128)(2,1)}, u32[]{:S(2)}, u32[]{:S(2)}) %collective-permute-start.4) | collective-permute-done | bytes 524320 | tf_op jit(solution)/shard_map/ppermute | solution.py:18
  148.7 1.1 constant_dynamic-update-slice_fusion.3
  149.8 1.1 constant_dynamic-update-slice_fusion.2
  150.9 1.1 constant_dynamic-update-slice_fusion.1
  152.0 1.2 fusion.44
  153.3 3.6 %reshape_squeeze.10 = bf16[1280,4,128]{2,1,0:T(4,128)(2,1)} reshape(bf16[1,1280,512]{2,1,0:T(8,128)(2,1)} %get-tuple-element.96) | data formatting | bytes 2621440 | tf_op jit(solution)/shard_map/reshape;squeeze | solution.py:76
  156.8 1.2 reshape_squeeze.11
  158.1 3.1 %copy_bitcast_fusion = (bf16[4,1280,128]{2,1,0:T(8,128)(2,1)}, bf16[4,1280,128]{2,1,0:T(8,128)(2,1)S(1)}) fusion(bf16[1280,4,128]{2,1,0:T(4,128)(2,1)} %reshape_squeeze.11, bf16[1280,4,128]{2,1,0:T(4,128)(2,1)} %reshape_squeeze.10), kind=kLoop, calls=%fused_computation.33 | loop fusion | bytes 5242880 | tf_op jit(solution)/shard_map/transpose | solution.py:77
  161.2 18.5 %while.11 = (s32[]{:T(128)}, bf16[4,4,256,128]{3,2,1,0:T(8,128)(2,1)S(1)}, bf16[4,4,256,128]{2,3,1,0:T(8,128)(2,1)S(1)}, bf16[4,1280,128]{2,1,0:T(8,128)(2,1)S(1...) while((s32[]{:T(128)}, ...), condition=%wide.region_8.9_spmd.clone, body=%wide.region_5.8_spmd.clone.sunk | while | flops 681506816 | bytes 17593436 | solution.py:94
  161.2 0.3 compare_and_fusion.2
  161.5 1.3 fusion.54
  162.8 1.0 fusion.55
  163.8 2.0 %fusion.56 = bf16[4,4,256,128]{3,2,1,0:T(8,128)(2,1)S(1)} fusion(bf16[4,4,256,128]{3,2,1,0:T(8,128)(2,1)S(1)} %get-tuple-element.166, s32[]{:T(128)} %get-tuple-element.165, f32[4,256,1280]{2,1,0:T(8,128)S(1)} %get-tuple-element.154, f32[4,256]{1,0:T(4,128)S(1)} %get-tuple-element.155, bf16[4,1280,128]{2,1,0:T(8,128)(2,1)} %get-tuple-element.178, ...), kind=kOutput, calls=%fused_computation.11.clone.1 | convolution fusion | flops 338427904 | bytes 5841920 | tf_op jit(solution)/shard_map/while/body/eval_jaxpr/dot_general | solution.py:90
  165.8 0.3 compare_and_fusion.2
  166.1 1.3 fusion.54
  167.4 1.0 fusion.55
  168.4 2.0 %fusion.56 = bf16[4,4,256,128]{3,2,1,0:T(8,128)(2,1)S(1)} fusion(bf16[4,4,256,128]{3,2,1,0:T(8,128)(2,1)S(1)} %get-tuple-element.166, s32[]{:T(128)} %get-tuple-element.165, f32[4,256,1280]{2,1,0:T(8,128)S(1)} %get-tuple-element.154, f32[4,256]{1,0:T(4,128)S(1)} %get-tuple-element.155, bf16[4,1280,128]{2,1,0:T(8,128)(2,1)} %get-tuple-element.178, ...), kind=kOutput, calls=%fused_computation.11.clone.1 | convolution fusion | flops 338427904 | bytes 5841920 | tf_op jit(solution)/shard_map/while/body/eval_jaxpr/dot_general | solution.py:90
  170.4 0.3 compare_and_fusion.2
  170.7 1.3 fusion.54
  172.0 1.0 fusion.55
  173.0 2.0 %fusion.56 = bf16[4,4,256,128]{3,2,1,0:T(8,128)(2,1)S(1)} fusion(bf16[4,4,256,128]{3,2,1,0:T(8,128)(2,1)S(1)} %get-tuple-element.166, s32[]{:T(128)} %get-tuple-element.165, f32[4,256,1280]{2,1,0:T(8,128)S(1)} %get-tuple-element.154, f32[4,256]{1,0:T(4,128)S(1)} %get-tuple-element.155, bf16[4,1280,128]{2,1,0:T(8,128)(2,1)} %get-tuple-element.178, ...), kind=kOutput, calls=%fused_computation.11.clone.1 | convolution fusion | flops 338427904 | bytes 5841920 | tf_op jit(solution)/shard_map/while/body/eval_jaxpr/dot_general | solution.py:90
  175.0 0.3 compare_and_fusion.2
  175.4 1.3 fusion.54
  176.7 1.0 fusion.55
  177.6 2.0 %fusion.56 = bf16[4,4,256,128]{3,2,1,0:T(8,128)(2,1)S(1)} fusion(bf16[4,4,256,128]{3,2,1,0:T(8,128)(2,1)S(1)} %get-tuple-element.166, s32[]{:T(128)} %get-tuple-element.165, f32[4,256,1280]{2,1,0:T(8,128)S(1)} %get-tuple-element.154, f32[4,256]{1,0:T(4,128)S(1)} %get-tuple-element.155, bf16[4,1280,128]{2,1,0:T(8,128)(2,1)} %get-tuple-element.178, ...), kind=kOutput, calls=%fused_computation.11.clone.1 | convolution fusion | flops 338427904 | bytes 5841920 | tf_op jit(solution)/shard_map/while/body/eval_jaxpr/dot_general | solution.py:90
  179.6 0.8 copy.19
  180.5 1.6 reshape.47
  (27 shorter events, 0.5 us)
Async XLA Ops:
  6.5 44.2 %all-reduce.3.cloned.1.call-start = ((), (), s32[]{:S(2)}) async-start(), calls=%async_computation.1 | async-start | bytes 1048576 | tf_op jit(solution)/shard_map/psum | solution.py:12
  11.0 61.8 %copy-start.3 = (bf16[2048]{0:T(1024)(128)(2,1)S(1)}, bf16[2048]{0:T(1024)(128)(2,1)}, u32[]{:S(2)}) copy-start(bf16[2048]{0:T(1024)(128)(2,1)} %param.10) | copy-start | bytes 12292
  11.0 61.8 %copy-start.4 = (s32[1,4]{1,0:T(1,128)S(1)}, s32[1,4]{1,0:T(1,128)}, u32[]{:S(2)}) copy-start(s32[1,4]{1,0:T(1,128)} %param.13) | copy-start | bytes 52
  11.0 62.0 %copy-start = (bf16[1,256,2048]{2,1,0:T(8,128)(2,1)S(1)}, bf16[1,256,2048]{2,1,0:T(8,128)(2,1)}, u32[]{:S(2)}) copy-start(bf16[1,256,2048]{2,1,0:T(8,128)(2,1)} %param.8) | copy-start | bytes 3145732
  11.1 92.2 %all-gather.2.cloned.1.call-start = ((), (), s32[]{:S(2)}) async-start(), calls=%async_computation | async-start | bytes 2359296 | tf_op jit(solution)/shard_map/all_gather | solution.py:65
  50.8 3.1 %collective-permute-start = (bf16[256,512]{1,0:T(8,128)(2,1)}, bf16[256,512]{1,0:T(8,128)(2,1)S(1)}, u32[]{:S(2)}, u32[]{:S(2)}) collective-permute-start(bf16[256,512]{1,0:T(8,128)(2,1)} %get-tuple-element.92), channel_id=1, source_target_pairs={{0,4},{4,0},{8,12},{12,8},{16,20},{20,16},{24,28},{28,24},{1,5},{5... | collective-permute-start | bytes 786440 | tf_op jit(solution)/shard_map/ppermute | solution.py:55
  55.1 16.0 %collective-permute-start.1 = (bf16[512,512]{1,0:T(8,128)(2,1)S(1)}, bf16[512,512]{1,0:T(8,128)(2,1)S(1)}, u32[]{:S(2)}, u32[]{:S(2)}) collective-permute-start(bf16[512,512]{1,0:T(8,128)(2,1)S(1)} %maximum_select_fusion.7), channel_id=1, source_target_pairs={{0,8},{4,12},{8,0},{12,4},{16,24},{20,28},{24,16},{28,20},{1,9},{5... | collective-permute-start | bytes 1572872 | tf_op jit(solution)/shard_map/ppermute | solution.py:55
  71.6 29.2 %collective-permute-start.2 = (bf16[1024,512]{1,0:T(8,128)(2,1)S(1)}, bf16[1024,512]{1,0:T(8,128)(2,1)}, u32[]{:S(2)}, u32[]{:S(2)}) collective-permute-start(bf16[1024,512]{1,0:T(8,128)(2,1)S(1)} %maximum_select_fusion.6), channel_id=1, source_target_pairs={{0,16},{4,20},{8,24},{12,28},{16,0},{20,4},{24,8},{28,12},{1,17},{... | collective-permute-start | bytes 3145736 | tf_op jit(solution)/shard_map/ppermute | solution.py:55
  103.2 2.5 %copy-start.1 = (bf16[1,256,512]{2,1,0:T(8,128)(2,1)}, bf16[1,256,512]{2,1,0:T(8,128)(2,1)S(1)}, u32[]{:S(2)}) copy-start(bf16[1,256,512]{2,1,0:T(8,128)(2,1)S(1)} %fusion.38) | copy-start | bytes 786436
  105.8 34.7 %collective-permute-start.3 = (bf16[2,256,512]{2,1,0:T(8,128)(2,1)S(1)}, bf16[2,256,512]{2,1,0:T(8,128)(2,1)}, u32[]{:S(2)}, u32[]{:S(2)}) collective-permute-start(bf16[2,256,512]{2,1,0:T(8,128)(2,1)S(1)} %pad_maximum_fusion), channel_id=1, source_target_pairs={{0,16},{4,20},{8,24},{12,28},{1,17},{5,21},{9,25},{13,29},{2,18},{... | collective-permute-start | bytes 1572872 | tf_op jit(solution)/shard_map/ppermute | solution.py:18
  109.7 39.0 %collective-permute-start.4 = (bf16[2,256,512]{2,1,0:T(8,128)(2,1)S(1)}, bf16[2,256,512]{2,1,0:T(8,128)(2,1)}, u32[]{:S(2)}, u32[]{:S(2)}) collective-permute-start(bf16[2,256,512]{2,1,0:T(8,128)(2,1)S(1)} %pad_maximum_fusion), channel_id=1, source_target_pairs={{0,12},{4,16},{8,20},{12,24},{16,28},{1,13},{5,17},{9,21},{13,25},... | collective-permute-start | bytes 1572872 | tf_op jit(solution)/shard_map/ppermute | solution.py:18
  113.0 36.8 %collective-permute-start.5 = (bf16[2,256,512]{2,1,0:T(8,128)(2,1)S(1)}, bf16[2,256,512]{2,1,0:T(8,128)(2,1)}, u32[]{:S(2)}, u32[]{:S(2)}) collective-permute-start(bf16[2,256,512]{2,1,0:T(8,128)(2,1)S(1)} %pad_maximum_fusion), channel_id=1, source_target_pairs={{0,8},{4,12},{8,16},{12,20},{16,24},{20,28},{1,9},{5,13},{9,17},{1... | collective-permute-start | bytes 1572872 | tf_op jit(solution)/shard_map/ppermute | solution.py:18
  116.1 34.7 %collective-permute-start.6 = (bf16[2,256,512]{2,1,0:T(8,128)(2,1)S(1)}, bf16[2,256,512]{2,1,0:T(8,128)(2,1)}, u32[]{:S(2)}, u32[]{:S(2)}) collective-permute-start(bf16[2,256,512]{2,1,0:T(8,128)(2,1)S(1)} %pad_maximum_fusion), channel_id=1, source_target_pairs={{0,4},{4,8},{8,12},{12,16},{16,20},{20,24},{24,28},{1,5},{5,9},{9,... | collective-permute-start | bytes 1572872 | tf_op jit(solution)/shard_map/ppermute | solution.py:18
  120.7 31.3 %copy-start.2 = (bf16[1,256,512]{2,1,0:T(8,128)(2,1)S(1)}, bf16[1,256,512]{2,1,0:T(8,128)(2,1)}, u32[]{:S(2)}) copy-start(bf16[1,256,512]{2,1,0:T(8,128)(2,1)} %copy-done.1) | copy-start | bytes 786436
Sparse Core Ops, SparseCore 0:
  11.2 39.5 all-reduce.2
  52.7 37.7 all-gather.1
